TPU v7x, 32 devices: a whole 2x2x4 slice. The times are simulated.
32 devices in a mesh: fact: 4 (over z), dim: 8 (over y, x, core).
Axes of the slice: x: 2, y: 2, z: 4, core: 2. Of those that a mesh axis runs over, the one named last changes fastest.
Arguments:
- facts: bfloat16 [4096, 512], P(('fact', 'dim')), may hold values from -6 to 6
- dims: bfloat16 [4096, 512], P(('fact', 'dim')), may hold values from -6 to 6
- tiles: bfloat16 [1024, 128, 128], P(('fact', 'dim')), may hold values from -0.125 to 0.125
- links: int32 [1024, 2], P(('fact', 'dim')), may hold values from 0 to 31, as said below
- link_count: int32 [32], P(('fact', 'dim')), may hold values from 8 to 32, as said below
- block_table: int32 [32], replicated, may hold values from 0 to 2
- w_self: bfloat16 [512, 512], replicated, may hold values from -0.25 to 0.25
- w_tables: bfloat16 [3, 512, 512], replicated, may hold values from -0.25 to 0.25
- cot: bfloat16 [4096, 512], P(('fact', 'dim')), may hold values from -6 to 6
Outputs:
- fact_out: bfloat16 [4096, 512], P(('fact', 'dim'))
- grad_dims: float32 [4096, 512], P(('fact', 'dim'))
- grad_w_self: float32 [512, 512], replicated
- grad_w_tables: float32 [3, 512, 512], replicated
Inputs may be any that keep to these rules, and one draw needn't show every extreme that they name: On device k = f * 8 + d (f, d its fact and dim indices), links[l,0] is a fact block among those of rows f * 128 * 8 to (f + 1) * 128 * 8 - 1, and links[l,1] is a dimension block held by a device with dim index d, i.e. links[l,1] % 8 == d. Slots beyond the device's count hold such indices too and are padding. `link_count`: some device has all 32 slots live and some device exactly 8.
All inputs are finite; a program needn't handle non-finite values.
Results may differ from a plain program's by a relative error of at most 0.017.
Values may be sent and summed in bfloat16 or wider, within the bound.
A program may use at most 64 MiB of HBM per device.

v0:
```python
import math

import jax
import jax.numpy as jnp
from jax import lax
from jax.sharding import PartitionSpec as P


def project_rows(rows, row_table, w_tables):
    acc = jnp.zeros((rows.shape[0], w_tables.shape[2]), jnp.float32)
    for table in range(w_tables.shape[0]):
        term = jnp.dot(rows, w_tables[table], preferred_element_type=jnp.float32)
        acc = acc + jnp.where(row_table[:, None] == table, term, jnp.float32(0.0))
    return acc.astype(jnp.bfloat16)


def lookup_tables(global_blocks, block_table):
    every = jnp.arange(block_table.shape[0], dtype=jnp.int32)
    match = global_blocks[:, None] == every[None, :]
    return jnp.sum(jnp.where(match, block_table[None, :], 0), axis=1)


def body(facts, dims, tiles, links, link_count, block_table, w_self, w_tables, cot):
    n_fact = lax.axis_size("fact")
    n_dim = lax.axis_size("dim")
    fact_pos = lax.axis_index("fact")
    dim_pos = lax.axis_index("dim")
    block = tiles.shape[1]
    width = facts.shape[1]
    rows_own = facts.shape[0]
    dim_own = dims.shape[0]
    link_slots = tiles.shape[0]
    tables = w_tables.shape[0]
    shard_rows = rows_own * n_dim
    panel_rows = dim_own * n_fact
    per_owner = dim_own // block
    own_blocks = (fact_pos * n_dim + dim_pos) * per_owner + jnp.arange(per_owner, dtype=jnp.int32)
    own_row_table = jnp.repeat(lookup_tables(own_blocks, block_table), block)
    panel_local = jnp.arange(n_fact * per_owner, dtype=jnp.int32)
    panel_blocks_global = (
        panel_local // per_owner * n_dim + dim_pos
    ) * per_owner + panel_local % per_owner
    panel_row_table = jnp.repeat(lookup_tables(panel_blocks_global, block_table), block)
    panel = project_rows(
        lax.all_gather(dims, "fact", axis=0, tiled=True), panel_row_table, w_tables
    )
    fact_blk = links[:, 0] - fact_pos * (shard_rows // block)
    global_dim = links[:, 1]
    holder = global_dim // per_owner // n_dim
    dim_blk = holder * per_owner + global_dim % per_owner
    live = (jnp.arange(link_slots, dtype=jnp.int32) < link_count[0]).astype(jnp.float32)
    group = math.gcd(link_slots, 32)
    steps_count = link_slots // group
    tile_groups = tiles.reshape(steps_count, group, block, block)
    fact_groups = fact_blk.reshape(steps_count, group)
    dim_groups = dim_blk.reshape(steps_count, group)
    live_groups = live.reshape(steps_count, group)
    panel_blocks = panel.reshape(panel_rows // block, block, width)

    def forward_step(acc, xs):
        tile, fact_ids, dim_ids, alive = xs
        contrib = jnp.einsum(
            "lij,ljd->lid", tile, panel_blocks[dim_ids], preferred_element_type=jnp.float32
        )
        return (acc.at[fact_ids].add(contrib * alive[:, None, None]), None)

    start_fwd = jnp.zeros((shard_rows // block, block, width), jnp.float32)
    partial_value, _ = lax.scan(
        forward_step, start_fwd, (tile_groups, fact_groups, dim_groups, live_groups)
    )
    agg = lax.psum_scatter(
        partial_value.reshape(shard_rows, width).astype(jnp.bfloat16),
        "dim",
        scatter_dimension=0,
        tiled=True,
    ).astype(jnp.float32)
    pre = jnp.dot(facts, w_self, preferred_element_type=jnp.float32) + agg
    fact_out = jax.nn.silu(pre).astype(jnp.bfloat16)
    sig = jax.nn.sigmoid(pre)
    grad_pre = (cot.astype(jnp.float32) * sig * (1.0 + pre * (1.0 - sig))).astype(jnp.bfloat16)
    total_facts = rows_own * n_fact * n_dim
    total_dims = dim_own * n_fact * n_dim
    grad_self = lax.dot_general(
        facts, grad_pre, (((0,), (0,)), ((), ())), preferred_element_type=jnp.float32
    ) * total_facts ** (-0.5)
    shard_grad = lax.all_gather(grad_pre, "dim", axis=0, tiled=True)
    grad_blocks = shard_grad.reshape(shard_rows // block, block, width)

    def backward_step(acc, xs):
        tile, fact_ids, dim_ids, alive = xs
        contrib = jnp.einsum(
            "lji,ljd->lid", tile, grad_blocks[fact_ids], preferred_element_type=jnp.float32
        )
        return (acc.at[dim_ids].add(contrib * alive[:, None, None]), None)

    start_bwd = jnp.zeros((panel_rows // block, block, width), jnp.float32)
    panel_grad, _ = lax.scan(
        backward_step, start_bwd, (tile_groups, fact_groups, dim_groups, live_groups)
    )
    own_grad = lax.psum_scatter(
        panel_grad.reshape(panel_rows, width).astype(jnp.bfloat16),
        "fact",
        scatter_dimension=0,
        tiled=True,
    )
    grad_dims = jnp.zeros((dim_own, width), jnp.float32)
    table_grads = []
    for table in range(tables):
        term = lax.dot_general(
            own_grad, w_tables[table], (((1,), (1,)), ((), ())), preferred_element_type=jnp.float32
        )
        grad_dims = grad_dims + jnp.where(own_row_table[:, None] == table, term, jnp.float32(0.0))
        masked = jnp.where(own_row_table[:, None] == table, dims, jnp.zeros_like(dims))
        table_grads.append(
            lax.dot_general(
                masked, own_grad, (((0,), (0,)), ((), ())), preferred_element_type=jnp.float32
            )
            * total_dims ** (-0.5)
        )
    grad_tab = jnp.stack(table_grads)
    grad_self, grad_tab = lax.psum((grad_self, grad_tab), ("fact", "dim"))
    return (fact_out, grad_dims, grad_self, grad_tab)


def solution(mesh):
    placed = (
        P(("fact", "dim"), None),
        P(("fact", "dim"), None),
        P(("fact", "dim"), None, None),
        P(("fact", "dim"), None),
        P(("fact", "dim")),
        P(),
        P(),
        P(),
        P(("fact", "dim"), None),
    )
    return jax.shard_map(
        body,
        mesh=mesh,
        in_specs=placed,
        out_specs=(P(("fact", "dim"), None), P(("fact", "dim"), None), P(), P()),
        check_vma=False,
    )
```

profile of v0, /device:TPU:0, one launch (start us, length us, event | category | flops | bytes accessed | tf_op | source)
XLA Modules:
  0.0 342.8 jit_solution(11924869971505833211)
XLA Ops:
  7.2 0.0 copy-start
  7.2 0.0 reduce-scatter.3.cloned.1.call-start
  7.3 0.9 select_reduce_fusion
  8.2 17.6 %all_gather.6 = bf16[512,512]{1,0:T(8,128)(2,1)S(1)} all-gather(bf16[128,512]{1,0:T(8,128)(2,1)} %param.10), channel_id=1, replica_groups=mesh['fact'=4,'dim'=8] {'fact'}, dimensions={0}, use_global_device_ids=true | all-gather | bytes 655360 | tf_op jit(solution)/shard_map/all_gather | solution.py:45
  25.8 0.1 broadcast_bitcast_fusion
  25.8 1.5 convolution_select_fusion
  27.3 2.5 convolution_select_fusion.1
  29.8 0.1 broadcast_bitcast_fusion.2
  30.5 1.8 fusion.6
  32.4 2.8 gather_fusion
  35.2 7.1 %multiply_bitcast_fusion.1 = f32[32,128,512]{1,2,0:T(8,128)} fusion(f32[32]{0:T(128)S(1)} %compare_convert_fusion, bf16[32,128,512]{2,1,0:T(8,128)(2,1)} %gather_fusion, bf16[32,128,128]{2,1,0:T(8,128)(2,1)S(1)} %copy-done), kind=kOutput, calls=%fused_computation.5 | convolution fusion | flops 538968064 | bytes 13631616 | tf_op jit(solution)/shard_map/while/body/eval_jaxpr/lij,ljd->lid/dot_general | solution.py:62
  42.2 9.0 %copy.22 = f32[32,128,512]{2,1,0:T(8,128)} copy(f32[32,128,512]{1,2,0:T(8,128)} %multiply_bitcast_fusion.1) | data formatting | bytes 16777216 | tf_op jit(solution)/shard_map/while/body/eval_jaxpr/mul | solution.py:65
  51.2 0.2 broadcast_in_dim.107
  51.5 11.8 %scatter_fusion = f32[8,128,512]{2,1,0:T(8,128)S(1)} fusion(f32[8,128,512]{2,1,0:T(8,128)S(1)} %broadcast_in_dim.107, s32[32]{0:T(128)S(1)} %get-tuple-element.63, f32[32,128,512]{2,1,0:T(8,128)} %copy.22), kind=kCustom, calls=%fused_computation.2 | custom fusion | flops 2097152 | bytes 25165952 | tf_op jit(solution)/shard_map/while/body/eval_jaxpr/scatter-add | solution.py:65
  63.2 0.0 copy-start.6
  63.3 0.0 copy-start.8
  63.3 1.1 convert_element_type.32
  64.4 0.0 reduce-scatter.3.cloned.1.call-update
  64.4 0.0 all-gather.2.cloned.1.call-start
  64.5 37.8 %reduce-scatter.3.cloned.1.call-done = bf16[128,512]{1,0:T(8,128)(2,1)} async-done(((bf16[1024,512]{1,0:T(8,128)(2,1)}), bf16[128,512]{1,0:T(8,128)(2,1)}) %reduce-scatter.3.cloned.1.call-update) | async-done | bytes 131088 | tf_op jit(solution)/shard_map/reduce_scatter | solution.py:71
  102.2 2.1 multiply_convert_fusion
  104.3 0.0 all-gather.2.cloned.1.call-update
  104.4 0.0 reduce-scatter.5.cloned.1.call-start
  104.4 23.7 %all-gather.2.cloned.1.call-done = bf16[1024,512]{1,0:T(8,128)(2,1)} async-done(((bf16[128,512]{1,0:T(8,128)(2,1)}), bf16[1024,512]{1,0:T(8,128)(2,1)}) %all-gather.2.cloned.1.call-update) | async-done | bytes 1048592 | tf_op jit(solution)/shard_map/all_gather | solution.py:86
  128.1 4.0 %gather_fusion.1 = bf16[32,128,512]{2,1,0:T(8,128)(2,1)} fusion(bf16[8,128,512]{2,1,0:T(8,128)(2,1)} %bitcast.61, s32[1024]{0:T(1024)S(1)} %pad_clamp_fusion), kind=kCustom, calls=%fused_computation.1 | custom fusion | bytes 8388736 | tf_op jit(solution)/shard_map/while/body/eval_jaxpr/gather | solution.py:92
  132.1 7.1 %multiply_bitcast_fusion = f32[32,128,512]{1,2,0:T(8,128)} fusion(f32[32]{0:T(128)S(1)} %compare_convert_fusion, bf16[32,128,512]{2,1,0:T(8,128)(2,1)} %gather_fusion.1, bf16[32,128,128]{2,1,0:T(8,128)(2,1)S(1)} %copy-done), kind=kOutput, calls=%fused_computation.4 | convolution fusion | flops 538968064 | bytes 13631616 | tf_op jit(solution)/shard_map/while/body/eval_jaxpr/lji,ljd->lid/dot_general | solution.py:91
  139.2 9.0 %copy.24 = f32[32,128,512]{2,1,0:T(8,128)} copy(f32[32,128,512]{1,2,0:T(8,128)} %multiply_bitcast_fusion) | data formatting | bytes 16777216 | tf_op jit(solution)/shard_map/while/body/eval_jaxpr/mul | solution.py:94
  148.2 0.1 broadcast_in_dim.119
  148.3 0.0 copy-start.4
  148.3 11.7 %scatter_fusion.1 = f32[4,128,512]{2,1,0:T(8,128)S(1)} fusion(f32[4,128,512]{2,1,0:T(8,128)S(1)} %broadcast_in_dim.119, s32[32]{0:T(128)S(1)} %get-tuple-element.62, f32[32,128,512]{2,1,0:T(8,128)} %copy.24), kind=kCustom, calls=%fused_computation.3 | custom fusion | flops 2097152 | bytes 25165952 | tf_op jit(solution)/shard_map/while/body/eval_jaxpr/scatter-add | solution.py:94
  160.0 0.9 convert_element_type.38
  160.9 0.0 reduce-scatter.5.cloned.1.call-update
  160.9 0.0 all-reduce.3.cloned.1.call-start
  161.0 0.6 fusion.30
  163.6 1.3 fusion.3
  164.8 18.1 %reduce-scatter.5.cloned.1.call-done = bf16[128,512]{1,0:T(8,128)(2,1)} async-done(((bf16[512,512]{1,0:T(8,128)(2,1)}), bf16[128,512]{1,0:T(8,128)(2,1)}) %reduce-scatter.5.cloned.1.call-update) | async-done | bytes 131088 | tf_op jit(solution)/shard_map/reduce_scatter | solution.py:100
  182.9 1.2 fusion
  184.1 1.2 fusion.1
  185.4 1.2 fusion.2
  186.6 0.0 copy-start.3
  186.6 2.0 pad_maximum_fusion
  188.6 0.0 all-reduce.3.cloned.1.call-update
  188.6 0.3 convolution_select_fusion.4
  188.9 0.3 fusion.7
  189.3 1.0 fusion.8
  190.3 139.5 %all-reduce.3.cloned.1.call-done = (f32[512,512]{0,1:T(8,128)}, f32[3,512,512]{2,1,0:T(8,128)}) async-done(((f32[512,512]{0,1:T(8,128)}, f32[3,512,512]{2,1,0:T(8,128)}), (f32[512,512]{0,1:T(8,128)}, f32[3,512,512]{2,1,0:T(8,128)})) %all-reduce.3.cloned.1.call-update) | async-done | bytes 4194320 | tf_op jit(solution)/shard_map/psum | solution.py:121
  329.8 2.6 copy.25
  332.4 3.9 %copy.33 = f32[3,512,512]{2,1,0:T(8,128)} copy(f32[3,512,512]{2,1,0:T(8,128)} %get-tuple-element.72) | data formatting | bytes 6291456
  (21 shorter events, 0.1 us)
Async XLA Ops:
  7.2 28.0 %copy-start = (bf16[32,128,128]{2,1,0:T(8,128)(2,1)S(1)}, bf16[32,128,128]{2,1,0:T(8,128)(2,1)}, u32[]{:S(2)}) copy-start(bf16[32,128,128]{2,1,0:T(8,128)(2,1)} %param.11) | copy-start | bytes 3145732
  7.2 22.7 %copy-start.7 = (s32[32,2]{0,1:T(2,128)S(1)}, s32[32,2]{0,1:T(2,128)}, u32[]{:S(2)}) copy-start(s32[32,2]{0,1:T(2,128)} %param.12) | copy-start | bytes 772
  7.2 95.0 %reduce-scatter.3.cloned.1.call-start = ((), (), s32[]{:S(2)}) async-start(), calls=%async_computation.2 | async-start | bytes 1179648 | tf_op jit(solution)/shard_map/reduce_scatter | solution.py:71
  63.2 39.0 %copy-start.6 = (bf16[128,512]{1,0:T(8,128)(2,1)S(1)}, bf16[128,512]{1,0:T(8,128)(2,1)}, u32[]{:S(2)}) copy-start(bf16[128,512]{1,0:T(8,128)(2,1)} %param.9) | copy-start | bytes 393220
  63.3 39.0 %copy-start.8 = (bf16[128,512]{1,0:T(8,128)(2,1)S(1)}, bf16[128,512]{1,0:T(8,128)(2,1)}, u32[]{:S(2)}) copy-start(bf16[128,512]{1,0:T(8,128)(2,1)} %param.17) | copy-start | bytes 393220
  64.4 63.7 %all-gather.2.cloned.1.call-start = ((), (), s32[]{:S(2)}) async-start(), calls=%async_computation.3 | async-start | bytes 1179648 | tf_op jit(solution)/shard_map/all_gather | solution.py:86
  104.4 78.5 %reduce-scatter.5.cloned.1.call-start = ((), (), s32[]{:S(2)}) async-start(), calls=%async_computation.4 | async-start | bytes 655360 | tf_op jit(solution)/shard_map/reduce_scatter | solution.py:100
  148.3 12.7 %copy-start.9 = (s32[32]{0:T(128)S(1)}, s32[32]{0:T(128)}, u32[]{:S(2)}) copy-start(s32[32]{0:T(128)} %param.14) | copy-start | bytes 388
  148.3 15.2 %copy-start.5 = (bf16[128,512]{1,0:T(8,128)(2,1)S(1)}, bf16[128,512]{1,0:T(8,128)(2,1)}, u32[]{:S(2)}) copy-start(bf16[128,512]{1,0:T(8,128)(2,1)} %get-tuple-element.60) | copy-start | bytes 393220
  148.3 34.6 %copy-start.4 = (bf16[128,512]{1,0:T(8,128)(2,1)S(1)}, bf16[128,512]{1,0:T(8,128)(2,1)}, u32[]{:S(2)}) copy-start(bf16[128,512]{1,0:T(8,128)(2,1)} %param.10) | copy-start | bytes 393220
  160.9 168.9 %all-reduce.3.cloned.1.call-start = ((), (), s32[]{:S(2)}) async-start(), calls=%async_computation.5 | async-start | bytes 8388608 | tf_op jit(solution)/shard_map/psum | solution.py:121
  186.6 2.0 copy-start.2
  186.6 2.0 copy-start.3
  329.8 6.5 %copy-start.1 = (bf16[32,128,128]{2,1,0:T(8,128)(2,1)S(1)}, bf16[32,128,128]{2,1,0:T(8,128)(2,1)}, u32[]{:S(2)}) copy-start(bf16[32,128,128]{2,1,0:T(8,128)(2,1)} %param.11) | copy-start | bytes 3145732
Sparse Core Ops, SparseCore 0:
  64.5 37.6 reduce-scatter.2
  104.7 23.3 all-gather.1
  161.0 21.8 reduce-scatter.4
  189.1 140.6 all-reduce.2
where the time goes:
time: 344 us; the launch traced here: 343 us
  waiting for transfers between devices  219 us (64%)
  local copies, waits for them, and re-layouts  31.8 us (9%)
  other arithmetic  29 us (8%)
  matrix products  28.6 us (8%)
  blocking collectives  17.6 us (5%)
  between operations  16.6 us (5%)
    psum x1, waiting for transfers between devices, body(): grad_self, grad_tab = lax.psum((grad_self, grad_tab), ('fact', 'dim'))  140 us
    reduce_scatter x1, waiting for transfers between devices, body(): lax.psum_scatter(partial_value.reshape(shard_rows, width).astype(jnp.bflo...  37.8 us
    all_gather x1, waiting for transfers between devices, body(): shard_grad = lax.all_gather(grad_pre, 'dim', axis=0, tiled=True)  23.7 us
    reduce_scatter x1, waiting for transfers between devices, body(): lax.psum_scatter(panel_grad.reshape(panel_rows, width).astype(jnp.bfloat1...  18.1 us
    all_gather x1, blocking collectives, body(): lax.all_gather(dims, 'fact', axis=0, tiled=True)  17.6 us
    scatter-add x1, other arithmetic, forward_step(): return (acc.at[fact_ids].add(contrib * alive[:, None, None]), None)  11.8 us
    scatter-add x1, other arithmetic, backward_step(): return (acc.at[dim_ids].add(contrib * alive[:, None, None]), None)  11.7 us
    mul x1, local copies, waits for them, and re-layouts, forward_step(): return (acc.at[fact_ids].add(contrib * alive[:, None, None]), None)  9 us
  transfers between devices with their start and end apart: 4, of which 4 were waited for; matrix products, arithmetic and copies ran while one was open for 1% of the time, Pallas kernels for 0%

commit v1 on v0

v1 whole, which is shorter than its diff:
```python
import functools

import jax
import jax.numpy as jnp
from jax import lax
from jax.experimental import pallas as pl
from jax.experimental.pallas import tpu as pltpu
from jax.sharding import PartitionSpec as P

MESH = pl.DeviceIdType.MESH
BF = jnp.bfloat16
F32 = jnp.float32
CORES = 2


def dot(a, b):
    return jnp.dot(a, b, preferred_element_type=F32)


def flip(x):
    return x.astype(F32).T.astype(BF)


def prep_kernel(dims_n, links, count, table, tiles, facts, dims, w_tables, adj, proj, chunks, acc):
    n_fact, n_dim = dims_n
    chips = n_dim // CORES
    block = tiles.shape[1]
    f = lax.axis_index("fact")
    d = lax.axis_index("dim")
    acc[...] = jnp.zeros_like(acc)
    own = table[f * n_dim + d]
    proj[...] = dot(dims[...], w_tables[own]).astype(BF)

    def add(l, _):
        i = links[l, 0] - f * n_dim
        row = lax.rem(i, CORES) * chips + lax.div(i, CORES)
        col = lax.div(links[l, 1], n_dim)
        acc[row, col] += tiles[l].astype(F32)
        return 0

    lax.fori_loop(0, count[0], add, 0)
    depth = chunks.shape[1] // 2
    facts_t = flip(facts[...])
    dims_t = flip(dims[...])
    for c in range(chips):
        chunks[c, :depth] = facts_t[c * depth : (c + 1) * depth]
        chunks[c, depth:] = dims_t[c * depth : (c + 1) * depth]
    for i in range(n_dim):
        for j in range(n_fact):
            adj[i * block : (i + 1) * block, j * block : (j + 1) * block] = acc[i, j].astype(BF)


def main_kernel(
    dims_n, table, adj, proj, chunks, facts, cot, w_self, w_tables,
    fact_out, grad_dims, weights,
    panel, adj_t, chunk_all, masked, pre, send1, recv1, mine, send2, recv2, gp, grad,
    send3, recv3, gs, gs_all, w_own, w_send, w_recv,
    a_s, a_r, f_s, f_r, b1_s, b1_r, b2_s, b2_r, c_s, c_r, cp_s, cp_r,
    d_s, d_r, e_s, e_r, w_s, w_r, z_s, z_r, p_s, p_r, q_s, q_r,
):
    n_fact, n_dim = dims_n
    chips = n_dim // CORES
    rows, width = facts.shape
    half = width // CORES
    depth = chunks.shape[1] // 2
    tables = w_tables.shape[0]
    per = n_fact // (tables + 1)
    part = depth // per
    f = lax.axis_index("fact")
    d = lax.axis_index("dim")
    c = lax.div(d, CORES)
    k = lax.rem(d, CORES)
    o = 1 - k
    mate = c * CORES + o
    scale_f = float(rows * n_fact * n_dim) ** -0.5
    started = []

    def send(src, dst, ss, rs, df, dd):
        copy = pltpu.make_async_remote_copy(
            src_ref=src, dst_ref=dst, send_sem=ss, recv_sem=rs,
            device_id=(df, dd), device_id_type=MESH,
        )
        copy.start()
        started.append(copy)
        return copy

    def blk(i):
        return pl.ds(pl.multiple_of(i * rows, rows), rows)

    def up(base, j, n):
        return lax.rem(base + j, n)

    barrier = pltpu.get_barrier_semaphore()
    for j in range(1, n_dim):
        pl.semaphore_signal(barrier, inc=1, device_id=(f, up(d, j, n_dim)), device_id_type=MESH)
    for j in range(1, n_fact):
        pl.semaphore_signal(barrier, inc=1, device_id=(up(f, j, n_fact), d), device_id_type=MESH)
    pl.semaphore_wait(barrier, n_dim + n_fact - 2)

    far = sorted(range(1, n_fact), key=lambda j: abs(2 * j - n_fact))
    copies_a = {
        j: send(proj, panel.at[blk(f)], a_s.at[j], a_r.at[j], up(f, j, n_fact), d) for j in far
    }
    rb = k * chips + c
    copies_f = {}
    for j in range(1, n_dim):
        to = up(d, j, n_dim)
        copies_f[j] = send(
            chunks.at[lax.div(to, CORES)], chunk_all.at[:, blk(rb)], f_s.at[j], f_r.at[j], f, to
        )
    panel[blk(f), :] = proj[...]
    chunk_all[:, blk(rb)] = chunks[c]
    pre[...] = dot(facts[...], w_self[...])
    for i in range(n_dim):
        adj_t[:, i * rows : (i + 1) * rows] = flip(adj[i * rows : (i + 1) * rows, :])
    for j in copies_a:
        copies_a[j].wait_recv()

    group = chips * rows

    def grp(i):
        return pl.ds(pl.multiple_of(i * group, group), group)

    send1[...] = dot(adj[grp(o), :], panel[...]).astype(BF)
    order = list(range(1, chips)) + [0]
    copies_1 = {}
    for j in order:
        at = blk(up(c, j, chips))
        copies_1[j] = send(send1.at[at], recv1.at[at], b1_s.at[j], b1_r.at[j], f, mate)
    mine[...] = dot(adj[grp(k), :], panel[...])
    copies_2 = {}
    for j in order:
        copies_1[j].wait_recv()
        chip = up(c, j, chips)
        total = mine[blk(chip), :] + recv1[blk(chip), :].astype(F32)
        if j:
            send2[j] = total.astype(BF)
            copies_2[j] = send(
                send2.at[j], recv2.at[j], b2_s.at[j], b2_r.at[j], f, chip * CORES + k
            )
        else:
            pre[...] += total
    for j in range(n_dim - 1, 0, -1):
        copies_f[j].wait_recv()
    for i in range(n_dim):
        source = lax.rem(i, chips) * CORES + i // chips
        name = table[f * n_dim + source]
        lanes = slice(i * rows, (i + 1) * rows)
        values = chunk_all[depth:, lanes].astype(F32)
        for t in range(tables):
            masked[t * depth : (t + 1) * depth, lanes] = (
                values * (name == t).astype(F32)
            ).astype(BF)
    total = pre[...]
    for j in range(1, chips):
        copies_2[j].wait_recv()
        total = total + recv2[j].astype(F32)
    sig = 1.0 / (1.0 + jnp.exp(-total))
    fact_out[...] = (total * sig).astype(BF)
    gp[blk(rb), :] = (cot[...].astype(F32) * sig * (1.0 + total * (1.0 - sig))).astype(BF)

    copies_c = {}
    for j in range(1, chips):
        copies_c[j] = send(
            gp.at[blk(rb)], gp.at[blk(rb)], c_s.at[j], c_r.at[j], f, up(c, j, chips) * CORES + k
        )
    copies_m = [send(gp.at[blk(rb)], gp.at[blk(rb)], cp_s.at[0], cp_r.at[0], f, mate)]
    for j in range(1, chips):
        copies_c[j].wait_recv()
        at = blk(k * chips + up(c, chips - j, chips))
        copies_m.append(send(gp.at[at], gp.at[at], cp_s.at[j], cp_r.at[j], f, mate))
    grad[...] = dot(adj_t[:, grp(k)], gp[grp(k), :])
    for copy in copies_m:
        copy.wait_recv()
    grad[...] += dot(adj_t[:, grp(o)], gp[grp(o), :])
    copies_d = {}
    for j in far:
        to = up(f, j, n_fact)
        send3[j] = grad[blk(to), :].astype(BF)
        copies_d[j] = send(send3.at[j], recv3.at[j], d_s.at[j], d_r.at[j], to, d)
    side = pl.ds(pl.multiple_of(k * half, half), half)
    w_own[:depth, :] = dot(chunk_all[:depth, :], gp[:, side]) * scale_f
    total = grad[blk(f), :]
    for j in far:
        copies_d[j].wait_recv()
        total = total + recv3[j].astype(F32)
    rounded = total.astype(BF)
    for h in range(CORES):
        gs[h] = rounded[:, h * half : (h + 1) * half]
    copies_e = []
    for j in range(1, n_dim):
        to = up(d, j, n_dim)
        copies_e.append(
            send(gs.at[lax.rem(to, CORES)], gs_all.at[blk(rb)], e_s.at[j], e_r.at[j], f, to)
        )
    gs_all[blk(rb), :] = gs[k]
    own = table[f * n_dim + d]
    grad_dims[...] = lax.dot_general(
        rounded, w_tables[own], (((1,), (1,)), ((), ())), preferred_element_type=F32
    )
    for copy in copies_e:
        copy.wait_recv()
    w_own[depth:, :] = dot(masked[...], gs_all[...]) * scale_f

    def unit(i):
        return pl.ds(pl.multiple_of(i * part, part), part)

    copies_w = {}
    for j in far:
        to = up(f, j, n_fact)
        w_send[j] = w_own[unit(to), :].astype(BF)
        copies_w[j] = send(w_send.at[j], w_recv.at[j], w_s.at[j], w_r.at[j], to, d)
    total = w_own[unit(f), :]
    for j in far:
        copies_w[j].wait_recv()
        total = total + w_recv[j].astype(F32)

    def place(ff, cc, kk):
        return (
            lax.div(ff, per),
            pl.ds(pl.multiple_of(cc * depth + lax.rem(ff, per) * part, part), part),
            pl.ds(pl.multiple_of(kk * half, half), half),
        )

    home = place(f, c, k)
    weights[home] = total.astype(BF)

    def region(ff, cc, kk):
        return weights.at[place(ff, cc, kk)]

    copies_z, copies_p, copies_q = {}, {}, []

    def spread(i):
        src = region(up(f, n_fact - i, n_fact), c, k)
        for j in range(1, chips):
            copies_p[i, j] = send(
                src, src, p_s.at[i, j], p_r.at[i, j], f, up(c, j, chips) * CORES + k
            )
        copies_q.append(send(src, src, q_s.at[i, 0], q_r.at[i, 0], f, mate))

    for j in far:
        copies_z[j] = send(
            region(f, c, k), region(f, c, k), z_s.at[j], z_r.at[j], up(f, j, n_fact), d
        )
    spread(0)
    near = sorted(range(1, n_fact), key=lambda j: min(j, n_fact - j))
    for i in near:
        copies_z[i].wait_recv()
        spread(i)
    for i in [0] + near:
        for j in range(1, chips):
            copies_p[i, j].wait_recv()
            src = region(up(f, n_fact - i, n_fact), up(c, chips - j, chips), k)
            copies_q.append(send(src, src, q_s.at[i, j], q_r.at[i, j], f, mate))
    for copy in copies_q:
        copy.wait_recv()
    for copy in started:
        copy.wait_send()


def body(facts, dims, tiles, links, link_count, block_table, w_self, w_tables, cot):
    n_fact = lax.axis_size("fact")
    n_dim = lax.axis_size("dim")
    chips = n_dim // CORES
    rows, width = facts.shape
    block = tiles.shape[1]
    tables = w_tables.shape[0]
    depth = width // chips
    half = width // CORES
    part = depth * (tables + 1) // n_fact
    dims_n = (n_fact, n_dim)
    vmem = pl.BlockSpec(memory_space=pltpu.VMEM)
    smem = pl.BlockSpec(memory_space=pltpu.SMEM)
    adj, proj, chunks = pl.pallas_call(
        functools.partial(prep_kernel, dims_n),
        out_shape=(
            jax.ShapeDtypeStruct((n_dim * rows, n_fact * rows), BF),
            jax.ShapeDtypeStruct((rows, width), BF),
            jax.ShapeDtypeStruct((chips, 2 * depth, rows), BF),
        ),
        in_specs=[smem, smem, smem, vmem, vmem, vmem, vmem],
        out_specs=(vmem, vmem, vmem),
        scratch_shapes=[pltpu.VMEM((n_dim, n_fact, block, block), F32)],
    )(links, link_count, block_table, tiles, facts, dims, w_tables)
    dma = pltpu.SemaphoreType.DMA
    fact_out, grad_dims, weights = pl.pallas_call(
        functools.partial(main_kernel, dims_n),
        out_shape=(
            jax.ShapeDtypeStruct((rows, width), BF),
            jax.ShapeDtypeStruct((rows, width), F32),
            jax.ShapeDtypeStruct((tables + 1, width, width), BF),
        ),
        in_specs=[smem] + [vmem] * 7,
        out_specs=(vmem, vmem, vmem),
        scratch_shapes=[
            pltpu.VMEM((n_fact * rows, width), BF),
            pltpu.VMEM((n_fact * rows, n_dim * rows), BF),
            pltpu.VMEM((2 * depth, n_dim * rows), BF),
            pltpu.VMEM((tables * depth, n_dim * rows), BF),
            pltpu.VMEM((rows, width), F32),
            pltpu.VMEM((chips * rows, width), BF),
            pltpu.VMEM((chips * rows, width), BF),
            pltpu.VMEM((chips * rows, width), F32),
            pltpu.VMEM((chips, rows, width), BF),
            pltpu.VMEM((chips, rows, width), BF),
            pltpu.VMEM((n_dim * rows, width), BF),
            pltpu.VMEM((n_fact * rows, width), F32),
            pltpu.VMEM((n_fact, rows, width), BF),
            pltpu.VMEM((n_fact, rows, width), BF),
            pltpu.VMEM((CORES, rows, half), BF),
            pltpu.VMEM((n_dim * rows, half), BF),
            pltpu.VMEM(((tables + 1) * depth, half), F32),
            pltpu.VMEM((n_fact, part, half), BF),
            pltpu.VMEM((n_fact, part, half), BF),
            dma((n_fact,)), dma((n_fact,)),
            dma((n_dim,)), dma((n_dim,)),
            dma((chips,)), dma((chips,)),
            dma((chips,)), dma((chips,)),
            dma((chips,)), dma((chips,)),
            dma((chips,)), dma((chips,)),
            dma((n_fact,)), dma((n_fact,)),
            dma((n_dim,)), dma((n_dim,)),
            dma((n_fact,)), dma((n_fact,)),
            dma((n_fact,)), dma((n_fact,)),
            dma((n_fact, chips)), dma((n_fact, chips)),
            dma((n_fact, chips)), dma((n_fact, chips)),
        ],
        compiler_params=pltpu.CompilerParams(collective_id=0, has_side_effects=True),
    )(block_table, adj, proj, chunks, facts, cot, w_self, w_tables)
    return fact_out, grad_dims, weights[0].astype(F32), weights[1:].astype(F32)


def solution(mesh):
    rows = P(("fact", "dim"), None)
    placed = (
        rows,
        rows,
        P(("fact", "dim"), None, None),
        rows,
        P(("fact", "dim")),
        P(),
        P(),
        P(),
        rows,
    )
    return jax.shard_map(
        body,
        mesh=mesh,
        in_specs=placed,
        out_specs=(rows, rows, P(), P()),
        check_vma=False,
    )
```

time: 344 us -> 98.6 us (0.29)
  waiting for transfers between devices: 219 us -> 0 us
  Pallas kernels: 0 us -> 88.8 us
  local copies, waits for them, and re-layouts: 31.8 us -> 2.73 us
  matrix products: 28.6 us -> 0 us
  other arithmetic: 29 us -> 5.71 us
  blocking collectives: 17.6 us -> 0 us
  between operations: 16.6 us -> 1.29 us
    psum x1 -> x0, waiting for transfers between devices: 140 us -> none  [body(): grad_self, grad_tab = lax.psum((grad_self, grad_tab), ('fact', 'dim'))]
    pallas_call x0 -> x2, Pallas kernels: none -> 88.8 us  [the longest x1 85.2 us: body(): pl.pallas_call(functools.partial(main_kernel, dims_n), out_shape=(jax.Sha...]
    reduce_scatter x2 -> x0, waiting for transfers between devices: 55.8 us -> none  [the longest x1 37.8 us: body(): lax.psum_scatter(partial_value.reshape(shard_rows, width).astype(jnp.bflo...]
    dot_general x13 -> x0, matrix products: 28.6 us -> none  [the longest x1 7.07 us: backward_step(): jnp.einsum('lji,ljd->lid', tile, grad_blocks[fact_ids], preferred_element...]
    all_gather x1 -> x0, waiting for transfers between devices: 23.7 us -> none  [body(): shard_grad = lax.all_gather(grad_pre, 'dim', axis=0, tiled=True)]
    scatter-add x2 -> x0, other arithmetic: 23.4 us -> none  [the longest x1 11.8 us: forward_step(): return (acc.at[fact_ids].add(contrib * alive[:, None, None]), None)]
    mul x2 -> x0, local copies, waits for them, and re-layouts: 18 us -> none  [the longest x1 9 us: forward_step(): return (acc.at[fact_ids].add(contrib * alive[:, None, None]), None)]
    all_gather x1 -> x0, blocking collectives: 17.6 us -> none  [body(): lax.all_gather(dims, 'fact', axis=0, tiled=True)]
  transfers between devices with their start and end apart: 4 -> 0, of which waited for: 4 -> 0; matrix products, arithmetic and copies ran while one was open for 1% -> 0% of each run, Pallas kernels for 0% -> 0%
where the time goes in v1:
time: 98.6 us; the launch traced here: 98.5 us
  Pallas kernels  88.8 us (90%)
  other arithmetic  5.71 us (6%)
  local copies, waits for them, and re-layouts  2.73 us (3%)
  between operations  1.29 us (1%)
    pallas_call x1, Pallas kernels, body(): pl.pallas_call(functools.partial(main_kernel, dims_n), out_shape=(jax.Sha...  85.2 us
    pallas_call x1, Pallas kernels, body(): pl.pallas_call(functools.partial(prep_kernel, dims_n), out_shape=(jax.Sha...  3.57 us
    convert_element_type x1, other arithmetic, body(): weights[1:].astype(F32)  3.56 us
    unnamed x7, local copies, waits for them, and re-layouts  2.73 us
    convert_element_type x1, other arithmetic, body(): weights[0].astype(F32)  2.15 us

profile of v1, /device:TPU:0, one launch (start us, length us, event | category | flops | bytes accessed | tf_op | source)
XLA Modules:
  0.0 98.5 jit_solution(8870127922867832581)
XLA Ops:
  1.3 1.4 %copy.13.links = s32[32,2]{1,0:T(8,128)} copy(s32[32,2]{0,1:T(2,128)} %param.12) | data formatting | bytes 512 | tf_op args[3]
  2.6 3.6 %shard_map.120 = (bf16[1024,512]{1,0:T(8,128)(2,1)}, bf16[128,512]{1,0:T(8,128)(2,1)}, bf16[4,256,128]{2,1,0:T(8,128)(2,1)}) custom-call(s32[32,2]{1,0:T(8,128)} %copy.13.links, s32[1]{0:T(128)S(6)} %copy.16.count, s32[32]{0:T(128)} %table.3, bf16[32,128,128]{2,1,0:T(8,128)(2,1)} %tiles.1, bf16[128,512]{1,0:T(8,128)(2,1)} %facts.3, bf16[128,512]{1,0:T(8,128)(2,1)} %dims.1, ...), custom_call_target="tpu_custom_call" | custom-call | tf_op jit(solution)/shard_map/pallas_call | solution.py:274
  6.2 85.2 %shard_map.121 = (bf16[128,512]{1,0:T(8,128)(2,1)}, f32[128,512]{1,0:T(8,128)}, bf16[4,512,512]{2,1,0:T(8,128)(2,1)}) custom-call(s32[32]{0:T(128)} %table.3, bf16[1024,512]{1,0:T(8,128)(2,1)} %get-tuple-element.10.adj, bf16[128,512]{1,0:T(8,128)(2,1)} %get-tuple-element.11.proj, bf16[4,256,128]{2,1,0:T(8,128)(2,1)} %get-tuple-element.12.chunks, ...), custom_call_target="tpu_custom_call" | custom-call | tf_op jit(solution)/shard_map/pallas_call | solution.py:286
  91.4 2.1 %bitcast_convert_fusion = f32[512,512]{1,0:T(8,128)} fusion(bf16[4,512,512]{2,1,0:T(8,128)(2,1)} %get-tuple-element.15), kind=kLoop, calls=%fused_computation.1 | loop fusion | flops 262144 | bytes 1572864 | tf_op jit(solution)/shard_map/convert_element_type | solution.py:330
  93.6 0.0 copy-start.1
  93.6 0.0 copy-start
  93.6 3.6 %slice_convert_fusion = f32[3,512,512]{2,1,0:T(8,128)} fusion(bf16[4,512,512]{2,1,0:T(8,128)(2,1)} %get-tuple-element.15), kind=kLoop, calls=%fused_computation | loop fusion | flops 786432 | bytes 4718592 | tf_op jit(solution)/shard_map/convert_element_type | solution.py:330
  97.2 0.0 copy-done.1
  97.2 0.7 copy.17
  97.8 0.0 copy-done
  97.8 0.7 copy.18
Async XLA Ops:
  93.6 3.6 %copy-start.1 = (bf16[128,512]{1,0:T(8,128)(2,1)S(1)}, bf16[128,512]{1,0:T(8,128)(2,1)}, u32[]{:S(2)}) copy-start(bf16[128,512]{1,0:T(8,128)(2,1)} %get-tuple-element.20) | copy-start | bytes 393220
  93.6 4.2 %copy-start = (f32[128,512]{1,0:T(8,128)S(1)}, f32[128,512]{1,0:T(8,128)}, u32[]{:S(2)}) copy-start(f32[128,512]{1,0:T(8,128)} %get-tuple-element.21) | copy-start | bytes 786436

commit v2 on v1

v2 whole, which is shorter than its diff:
```python
import functools

import jax
import jax.numpy as jnp
from jax import lax
from jax.experimental import pallas as pl
from jax.experimental.pallas import tpu as pltpu
from jax.sharding import PartitionSpec as P

MESH = pl.DeviceIdType.MESH
BF = jnp.bfloat16
F32 = jnp.float32
CORES = 2
STAGES = 2


def dot(a, b):
    return jnp.dot(a, b, preferred_element_type=F32)


def flip(x):
    return x.astype(F32).T.astype(BF)


def prep_kernel(dims_n, links, count, table, tiles, facts, dims, w_tables, adj, proj, chunks, acc):
    n_fact, n_dim = dims_n
    chips = n_dim // CORES
    block = tiles.shape[1]
    f = lax.axis_index("fact")
    d = lax.axis_index("dim")
    acc[...] = jnp.zeros_like(acc)
    own = table[f * n_dim + d]
    both = dot(dims[...], w_tables[own]).astype(BF)
    cut = proj.shape[2]
    for h in range(proj.shape[0]):
        proj[h] = both[:, h * cut : (h + 1) * cut]

    def add(l, _):
        i = links[0, l] - f * n_dim
        row = lax.rem(i, CORES) * chips + lax.div(i, CORES)
        col = lax.div(links[1, l], n_dim)
        acc[row, col] += tiles[l].astype(F32)
        return 0

    lax.fori_loop(0, count[0], add, 0)
    depth = chunks.shape[1] // 2
    facts_t = flip(facts[...])
    dims_t = flip(dims[...])
    for c in range(chips):
        chunks[c, :depth] = facts_t[c * depth : (c + 1) * depth]
        chunks[c, depth:] = dims_t[c * depth : (c + 1) * depth]
    for i in range(n_dim):
        for j in range(n_fact):
            adj[i * block : (i + 1) * block, j * block : (j + 1) * block] = acc[i, j].astype(BF)


def main_kernel(
    dims_n, table, adj, proj, chunks, facts, cot, w_self, w_tables,
    fact_out, grad_dims, weights,
    panel, adj_t, chunk_all, masked, pre, send1, recv1, mine, send2, recv2, gp, grad,
    send3, recv3, gs, gs_all, w_own, w_send, w_recv,
    a_s, a_r, f_s, f_r, b1_s, b1_r, b2_s, b2_r, c_s, c_r, cp_s, cp_r,
    d_s, d_r, e_s, e_r, w_s, w_r, z_s, z_r, p_s, p_r, q_s, q_r,
):
    n_fact, n_dim = dims_n
    chips = n_dim // CORES
    rows, width = facts.shape
    cut = width // STAGES
    thin = cut // CORES
    depth = chunks.shape[1] // 2
    tables = w_tables.shape[0]
    per = n_fact // (tables + 1)
    part = depth // per
    f = lax.axis_index("fact")
    d = lax.axis_index("dim")
    c = lax.div(d, CORES)
    k = lax.rem(d, CORES)
    o = 1 - k
    mate = c * CORES + o
    scale_f = float(rows * n_fact * n_dim) ** -0.5
    started = []

    def send(src, dst, ss, rs, df, dd):
        copy = pltpu.make_async_remote_copy(
            src_ref=src, dst_ref=dst, send_sem=ss, recv_sem=rs,
            device_id=(df, dd), device_id_type=MESH,
        )
        copy.start()
        started.append(copy)
        return copy

    def blk(i):
        return pl.ds(pl.multiple_of(i * rows, rows), rows)

    def cols(h):
        return slice(h * cut, (h + 1) * cut)

    def up(base, j, n):
        return lax.rem(base + j, n)

    barrier = pltpu.get_barrier_semaphore()
    for j in range(1, n_dim):
        pl.semaphore_signal(barrier, inc=1, device_id=(f, up(d, j, n_dim)), device_id_type=MESH)
    for j in range(1, n_fact):
        pl.semaphore_signal(barrier, inc=1, device_id=(up(f, j, n_fact), d), device_id_type=MESH)
    pl.semaphore_wait(barrier, n_dim + n_fact - 2)

    far = sorted(range(1, n_fact), key=lambda j: abs(2 * j - n_fact))
    near = sorted(range(1, n_fact), key=lambda j: min(j, n_fact - j))
    every = range(STAGES)
    rb = k * chips + c
    copies_a = {}
    for h in every:
        for j in far:
            copies_a[h, j] = send(
                proj.at[h], panel.at[h, blk(f)], a_s.at[h, j], a_r.at[h, j], up(f, j, n_fact), d
            )
    copies_f = {}
    for j in range(1, n_dim):
        to = up(d, j, n_dim)
        copies_f[j] = send(
            chunks.at[lax.div(to, CORES)], chunk_all.at[:, blk(rb)], f_s.at[j], f_r.at[j], f, to
        )
    for h in every:
        panel[h, blk(f), :] = proj[h]
        pre[h] = dot(facts[...], w_self[:, cols(h)])
    chunk_all[:, blk(rb)] = chunks[c]
    for i in range(n_dim):
        adj_t[:, i * rows : (i + 1) * rows] = flip(adj[i * rows : (i + 1) * rows, :])

    group = chips * rows

    def grp(i):
        return pl.ds(pl.multiple_of(i * group, group), group)

    order = list(range(1, chips)) + [0]
    copies_1, copies_2, copies_c, copies_m = {}, {}, {}, {}

    def forward(h):
        for j in far:
            copies_a[h, j].wait_recv()
        send1[h] = dot(adj[grp(o), :], panel[h]).astype(BF)
        for j in order:
            at = blk(up(c, j, chips))
            copies_1[h, j] = send(
                send1.at[h, at], recv1.at[h, at], b1_s.at[h, j], b1_r.at[h, j], f, mate
            )
        mine[h] = dot(adj[grp(k), :], panel[h])

    def pair(h):
        for j in order:
            copies_1[h, j].wait_recv()
            chip = up(c, j, chips)
            total = mine[h, blk(chip), :] + recv1[h, blk(chip), :].astype(F32)
            if j:
                send2[h, j] = total.astype(BF)
                copies_2[h, j] = send(
                    send2.at[h, j], recv2.at[h, j], b2_s.at[h, j], b2_r.at[h, j],
                    f, chip * CORES + k,
                )
            else:
                pre[h] += total

    def activate(h):
        total = pre[h]
        for j in range(1, chips):
            copies_2[h, j].wait_recv()
            total = total + recv2[h, j].astype(F32)
        sig = 1.0 / (1.0 + jnp.exp(-total))
        gp[h, blk(rb), :] = (
            cot[:, cols(h)].astype(F32) * sig * (1.0 + total * (1.0 - sig))
        ).astype(BF)
        src = gp.at[h, blk(rb)]
        for j in range(1, chips):
            copies_c[h, j] = send(
                src, src, c_s.at[h, j], c_r.at[h, j], f, up(c, j, chips) * CORES + k
            )
        copies_m[h, 0] = send(src, src, cp_s.at[h, 0], cp_r.at[h, 0], f, mate)
        fact_out[:, cols(h)] = (total * sig).astype(BF)

    def share(h):
        for j in range(1, chips):
            copies_c[h, j].wait_recv()
            src = gp.at[h, blk(k * chips + up(c, chips - j, chips))]
            copies_m[h, j] = send(src, src, cp_s.at[h, j], cp_r.at[h, j], f, mate)

    def mask():
        for j in range(1, n_dim):
            copies_f[j].wait_recv()
        for i in range(n_dim):
            source = (i % chips) * CORES + i // chips
            name = table[f * n_dim + source]
            lanes = slice(i * rows, (i + 1) * rows)
            values = chunk_all[depth:, lanes].astype(F32)
            for t in range(tables):
                masked[t * depth : (t + 1) * depth, lanes] = (
                    values * (name == t).astype(F32)
                ).astype(BF)

    copies_d, copies_e, copies_w = {}, {}, {}

    def backward(h):
        grad[h] = dot(adj_t[:, grp(k)], gp[h, grp(k), :])
        for j in range(chips):
            copies_m[h, j].wait_recv()
        grad[h] += dot(adj_t[:, grp(o)], gp[h, grp(o), :])
        for j in far:
            to = up(f, j, n_fact)
            send3[h, j] = grad[h, blk(to), :].astype(BF)
            copies_d[h, j] = send(
                send3.at[h, j], recv3.at[h, j], d_s.at[h, j], d_r.at[h, j], to, d
            )

    side = pl.ds(pl.multiple_of(k * thin, thin), thin)

    def own_weight(h):
        w_own[h, :depth, :] = dot(chunk_all[:depth, :], gp[h, :, side]) * scale_f

    def collect(h):
        total = grad[h, blk(f), :]
        for j in near:
            copies_d[h, j].wait_recv()
            total = total + recv3[h, j].astype(F32)
        rounded = total.astype(BF)
        for i in range(CORES):
            gs[h, i] = rounded[:, i * thin : (i + 1) * thin]
        for j in range(1, n_dim):
            to = up(d, j, n_dim)
            copies_e[h, j] = send(
                gs.at[h, lax.rem(to, CORES)], gs_all.at[h, blk(rb)], e_s.at[h, j], e_r.at[h, j],
                f, to,
            )
        gs_all[h, blk(rb), :] = gs[h, k]
        own = table[f * n_dim + d]
        term = lax.dot_general(
            rounded, w_tables[own, :, cols(h)], (((1,), (1,)), ((), ())),
            preferred_element_type=F32,
        )
        if h:
            grad_dims[...] += term
        else:
            grad_dims[...] = term

    def unit(i):
        return pl.ds(pl.multiple_of(i * part, part), part)

    def table_weight(h):
        for j in range(1, n_dim):
            copies_e[h, j].wait_recv()
        w_own[h, depth:, :] = dot(masked[...], gs_all[h]) * scale_f
        for j in far:
            to = up(f, j, n_fact)
            w_send[h, j] = w_own[h, unit(to), :].astype(BF)
            copies_w[h, j] = send(
                w_send.at[h, j], w_recv.at[h, j], w_s.at[h, j], w_r.at[h, j], to, d
            )

    def place(h, ff, cc, kk):
        return (
            lax.div(ff, per),
            pl.ds(pl.multiple_of(cc * depth + lax.rem(ff, per) * part, part), part),
            pl.ds(pl.multiple_of(h * cut + kk * thin, thin), thin),
        )

    def region(h, ff, cc, kk):
        return weights.at[place(h, ff, cc, kk)]

    copies_z, copies_p, copies_q = {}, {}, []

    def spread(h, i):
        src = region(h, up(f, n_fact - i, n_fact), c, k)
        for j in range(1, chips):
            copies_p[h, i, j] = send(
                src, src, p_s.at[h, i, j], p_r.at[h, i, j], f, up(c, j, chips) * CORES + k
            )
        copies_q.append(send(src, src, q_s.at[h, i, 0], q_r.at[h, i, 0], f, mate))

    def finish(h):
        total = w_own[h, unit(f), :]
        for j in near:
            copies_w[h, j].wait_recv()
            total = total + w_recv[h, j].astype(F32)
        weights[place(h, f, c, k)] = total.astype(BF)
        src = region(h, f, c, k)
        for j in far:
            copies_z[h, j] = send(
                src, src, z_s.at[h, j], z_r.at[h, j], up(f, j, n_fact), d
            )
        spread(h, 0)

    def relay(h):
        for i in near:
            copies_z[h, i].wait_recv()
            spread(h, i)

    def hand(h):
        for i in [0] + near:
            for j in range(1, chips):
                copies_p[h, i, j].wait_recv()
                src = region(h, up(f, n_fact - i, n_fact), up(c, chips - j, chips), k)
                copies_q.append(send(src, src, q_s.at[h, i, j], q_r.at[h, i, j], f, mate))

    forward(0)
    pair(0)
    forward(1)
    activate(0)
    pair(1)
    mask()
    share(0)
    activate(1)
    backward(0)
    own_weight(0)
    share(1)
    backward(1)
    own_weight(1)
    collect(0)
    table_weight(0)
    collect(1)
    finish(0)
    table_weight(1)
    relay(0)
    finish(1)
    hand(0)
    relay(1)
    hand(1)
    for copy in copies_q:
        copy.wait_recv()
    for copy in started:
        copy.wait_send()


def post_kernel(cuts, out_in, dims_in, weights, fact_out, grad_dims, w_self, w_tables):
    step = pl.program_id(0)

    @pl.when(step == 0)
    def _():
        fact_out[...] = out_in[...]
        grad_dims[...] = dims_in[...]

    @pl.when(step < cuts)
    def _():
        w_self[...] = weights[0].astype(F32)

    @pl.when(step >= cuts)
    def _():
        w_tables[...] = weights[...].astype(F32)


def body(facts, dims, tiles, links, link_count, block_table, w_self, w_tables, cot):
    n_fact = lax.axis_size("fact")
    n_dim = lax.axis_size("dim")
    chips = n_dim // CORES
    rows, width = facts.shape
    block = tiles.shape[1]
    tables = w_tables.shape[0]
    depth = width // chips
    cut = width // STAGES
    thin = cut // CORES
    part = depth * (tables + 1) // n_fact
    dims_n = (n_fact, n_dim)
    vmem = pl.BlockSpec(memory_space=pltpu.VMEM)
    smem = pl.BlockSpec(memory_space=pltpu.SMEM)
    adj, proj, chunks = pl.pallas_call(
        functools.partial(prep_kernel, dims_n),
        out_shape=(
            jax.ShapeDtypeStruct((n_dim * rows, n_fact * rows), BF),
            jax.ShapeDtypeStruct((STAGES, rows, cut), BF),
            jax.ShapeDtypeStruct((chips, 2 * depth, rows), BF),
        ),
        in_specs=[smem, smem, smem, vmem, vmem, vmem, vmem],
        out_specs=(vmem, vmem, vmem),
        scratch_shapes=[pltpu.VMEM((n_dim, n_fact, block, block), F32)],
        name="prep",
    )(links.T, link_count, block_table, tiles, facts, dims, w_tables)

    def sems(*shape):
        return [pltpu.SemaphoreType.DMA((STAGES, *shape))] * 2

    fact_out, grad_dims, weights = pl.pallas_call(
        functools.partial(main_kernel, dims_n),
        out_shape=(
            jax.ShapeDtypeStruct((rows, width), BF),
            jax.ShapeDtypeStruct((rows, width), F32),
            jax.ShapeDtypeStruct((tables + 1, width, width), BF),
        ),
        in_specs=[smem] + [vmem] * 7,
        out_specs=(vmem, vmem, vmem),
        scratch_shapes=[
            pltpu.VMEM((STAGES, n_fact * rows, cut), BF),
            pltpu.VMEM((n_fact * rows, n_dim * rows), BF),
            pltpu.VMEM((2 * depth, n_dim * rows), BF),
            pltpu.VMEM((tables * depth, n_dim * rows), BF),
            pltpu.VMEM((STAGES, rows, cut), F32),
            pltpu.VMEM((STAGES, chips * rows, cut), BF),
            pltpu.VMEM((STAGES, chips * rows, cut), BF),
            pltpu.VMEM((STAGES, chips * rows, cut), F32),
            pltpu.VMEM((STAGES, chips, rows, cut), BF),
            pltpu.VMEM((STAGES, chips, rows, cut), BF),
            pltpu.VMEM((STAGES, n_dim * rows, cut), BF),
            pltpu.VMEM((STAGES, n_fact * rows, cut), F32),
            pltpu.VMEM((STAGES, n_fact, rows, cut), BF),
            pltpu.VMEM((STAGES, n_fact, rows, cut), BF),
            pltpu.VMEM((STAGES, CORES, rows, thin), BF),
            pltpu.VMEM((STAGES, n_dim * rows, thin), BF),
            pltpu.VMEM((STAGES, (tables + 1) * depth, thin), F32),
            pltpu.VMEM((STAGES, n_fact, part, thin), BF),
            pltpu.VMEM((STAGES, n_fact, part, thin), BF),
            *sems(n_fact),
            *[pltpu.SemaphoreType.DMA((n_dim,))] * 2,
            *sems(chips), *sems(chips), *sems(chips), *sems(chips),
            *sems(n_fact), *sems(n_dim), *sems(n_fact), *sems(n_fact),
            *sems(n_fact, chips), *sems(n_fact, chips),
        ],
        compiler_params=pltpu.CompilerParams(collective_id=0, has_side_effects=True),
        name="main",
    )(block_table, adj, proj, chunks, facts, cot, w_self, w_tables)
    cuts = CORES
    tall = width // cuts
    whole = pl.BlockSpec((rows, width), lambda i: (0, 0))
    return pl.pallas_call(
        functools.partial(post_kernel, cuts),
        out_shape=(
            jax.ShapeDtypeStruct((rows, width), BF),
            jax.ShapeDtypeStruct((rows, width), F32),
            jax.ShapeDtypeStruct((width, width), F32),
            jax.ShapeDtypeStruct((tables, width, width), F32),
        ),
        grid=((tables + 1) * cuts,),
        in_specs=[
            whole, whole, pl.BlockSpec((1, tall, width), lambda i: (i // cuts, i % cuts, 0))
        ],
        out_specs=(
            whole,
            whole,
            pl.BlockSpec((tall, width), lambda i: (jnp.minimum(i, cuts - 1), 0)),
            pl.BlockSpec(
                (1, tall, width),
                lambda i: (jnp.maximum(i // cuts - 1, 0), jnp.where(i < cuts, 0, i % cuts), 0),
            ),
        ),
        name="post",
    )(fact_out, grad_dims, weights)


def solution(mesh):
    rows = P(("fact", "dim"), None)
    placed = (
        rows,
        rows,
        P(("fact", "dim"), None, None),
        rows,
        P(("fact", "dim")),
        P(),
        P(),
        P(),
        rows,
    )
    return jax.shard_map(
        body,
        mesh=mesh,
        in_specs=placed,
        out_specs=(rows, rows, P(), P()),
        check_vma=False,
    )
```

time: 98.6 us -> 83.8 us (0.85)
  Pallas kernels: 88.8 us -> 81.9 us
  other arithmetic: 5.71 us -> 0 us
  local copies, waits for them, and re-layouts: 2.73 us -> 0 us
    pallas_call x1, Pallas kernels: 85.2 us -> 71.7 us  [body(): pl.pallas_call(functools.partial(main_kernel, dims_n), out_shape=(jax.Sha...]
    pallas_call x0 -> x1, Pallas kernels: none -> 6.54 us  [body(): pl.pallas_call(functools.partial(post_kernel, cuts), out_shape=(jax.Shape...]
    convert_element_type x2 -> x0, other arithmetic: 5.71 us -> none  [the longest x1 3.56 us: body(): weights[1:].astype(F32)]
    unnamed x7 -> x0, local copies, waits for them, and re-layouts: 2.73 us -> none
where the time goes in v2:
time: 83.8 us; the launch traced here: 83.2 us
  Pallas kernels  81.9 us (98%)
  between operations  1.29 us (2%)
    pallas_call x1, Pallas kernels, body(): pl.pallas_call(functools.partial(main_kernel, dims_n), out_shape=(jax.Sha...  71.7 us
    pallas_call x1, Pallas kernels, body(): pl.pallas_call(functools.partial(post_kernel, cuts), out_shape=(jax.Shape...  6.54 us
    pallas_call x1, Pallas kernels, body(): pl.pallas_call(functools.partial(prep_kernel, dims_n), out_shape=(jax.Sha...  3.64 us

profile of v2, /device:TPU:0, one launch (start us, length us, event | category | flops | bytes accessed | tf_op | source)
XLA Modules:
  0.0 83.2 jit_solution(7182955568562406315)
XLA Ops:
  1.3 3.6 %prep.1 = (bf16[1024,512]{1,0:T(8,128)(2,1)}, bf16[2,128,256]{2,1,0:T(8,128)(2,1)}, bf16[4,256,128]{2,1,0:T(8,128)(2,1)}) custom-call(s32[2,32]{1,0:T(2,128)} %bitcast.1, s32[1]{0:T(128)S(6)} %copy.13.count, s32[32]{0:T(128)} %table.3, bf16[32,128,128]{2,1,0:T(8,128)(2,1)} %tiles.1, bf16[128,512]{1,0:T(8,128)(2,1)} %facts.3, bf16[128,512]{1,0:T(8,128)(2,1)} %dims.1, ...), custom_call_target="tpu_custom_call" | custom-call | tf_op jit(solution)/shard_map/prep/pallas_call | solution.py:363
  4.9 71.7 %main.1 = (bf16[128,512]{1,0:T(8,128)(2,1)}, f32[128,512]{1,0:T(8,128)}, bf16[4,512,512]{2,1,0:T(8,128)(2,1)}) custom-call(s32[32]{0:T(128)} %table.3, bf16[1024,512]{1,0:T(8,128)(2,1)} %get-tuple-element.10.adj, bf16[2,128,256]{2,1,0:T(8,128)(2,1)} %get-tuple-element.11.proj, bf16[4,256,128]{2,1,0:T(8,128)(2,1)} %get-tuple-element.12.chunks, ...), custom_call_target="tpu_custom_call" | custom-call | tf_op jit(solution)/shard_map/main/pallas_call | solution.py:379
  76.7 6.5 %post.1 = (bf16[128,512]{1,0:T(8,128)(2,1)}, f32[128,512]{1,0:T(8,128)}, f32[512,512]{1,0:T(8,128)}, f32[3,512,512]{2,1,0:T(8,128)}) custom-call(bf16[128,512]{1,0:T(8,128)(2,1)} %get-tuple-element.13.out_in, f32[128,512]{1,0:T(8,128)} %get-tuple-element.14.dims_in, bf16[4,512,512]{2,1,0:T(8,128)(2,1)} %get-tuple-element.15.weights), custom_call_target="tpu_custom_call" | custom-call | tf_op jit(solution)/shard_map/post/pallas_call | solution.py:420

commit v3 on v2

--- a/solution.py
+++ b/solution.py
@@ -358,6 +358,10 @@
     thin = cut // CORES
     part = depth * (tables + 1) // n_fact
     dims_n = (n_fact, n_dim)
+    cells = n_fact * n_dim * rows * rows
+    panes = (n_fact + n_dim) * rows * width
+    grant = min(62 << 20, 4 * cells + 16 * panes + 8 * tables * width * width + (6 << 20))
+    small = min(62 << 20, 8 * cells + 4 * tables * width * width + (6 << 20))
     vmem = pl.BlockSpec(memory_space=pltpu.VMEM)
     smem = pl.BlockSpec(memory_space=pltpu.SMEM)
     adj, proj, chunks = pl.pallas_call(
@@ -370,6 +374,7 @@
         in_specs=[smem, smem, smem, vmem, vmem, vmem, vmem],
         out_specs=(vmem, vmem, vmem),
         scratch_shapes=[pltpu.VMEM((n_dim, n_fact, block, block), F32)],
+        compiler_params=pltpu.CompilerParams(vmem_limit_bytes=small),
         name="prep",
     )(links.T, link_count, block_table, tiles, facts, dims, w_tables)
 
@@ -411,7 +416,9 @@
             *sems(n_fact), *sems(n_dim), *sems(n_fact), *sems(n_fact),
             *sems(n_fact, chips), *sems(n_fact, chips),
         ],
-        compiler_params=pltpu.CompilerParams(collective_id=0, has_side_effects=True),
+        compiler_params=pltpu.CompilerParams(
+            collective_id=0, has_side_effects=True, vmem_limit_bytes=grant
+        ),
         name="main",
     )(block_table, adj, proj, chunks, facts, cot, w_self, w_tables)
     cuts = CORES
@@ -438,6 +445,7 @@
                 lambda i: (jnp.maximum(i // cuts - 1, 0), jnp.where(i < cuts, 0, i % cuts), 0),
             ),
         ),
+        compiler_params=pltpu.CompilerParams(vmem_limit_bytes=12 << 20),
         name="post",
     )(fact_out, grad_dims, weights)
 

time: 83.8 us -> 81.8 us (0.976)
  Pallas kernels: 81.9 us -> 74 us
  local copies, waits for them, and re-layouts: 0 us -> 6.02 us
    unnamed x0 -> x22, local copies, waits for them, and re-layouts: none -> 6.02 us
    pallas_call x1, Pallas kernels: 71.7 us -> 68.8 us  [body(): pl.pallas_call(functools.partial(main_kernel, dims_n), out_shape=(jax.Sha...]
    pallas_call x1, Pallas kernels: 6.54 us -> 3.93 us  [body(): pl.pallas_call(functools.partial(post_kernel, cuts), out_shape=(jax.Shape...]
    pallas_call x1, Pallas kernels: 3.64 us -> 1.3 us  [body(): pl.pallas_call(functools.partial(prep_kernel, dims_n), out_shape=(jax.Sha...]
where the time goes in v3:
time: 81.8 us; the launch traced here: 81.4 us
  Pallas kernels  74 us (90%)
  local copies, waits for them, and re-layouts  6.02 us (7%)
  between operations  1.34 us (2%)
    pallas_call x1, Pallas kernels, body(): pl.pallas_call(functools.partial(main_kernel, dims_n), out_shape=(jax.Sha...  68.8 us
    unnamed x22, local copies, waits for them, and re-layouts  6.02 us
    pallas_call x1, Pallas kernels, body(): pl.pallas_call(functools.partial(post_kernel, cuts), out_shape=(jax.Shape...  3.93 us

profile of v3, /device:TPU:0, one launch (start us, length us, event | category | flops | bytes accessed | tf_op | source)
XLA Modules:
  0.0 81.4 jit_solution(11550076715509505074)
XLA Ops:
  0.6 0.0 copy-start.9
  1.3 0.0 copy-start
  1.3 1.4 %copy-done = bf16[3,512,512]{2,1,0:T(8,128)(2,1)S(1)} copy-done((bf16[3,512,512]{2,1,0:T(8,128)(2,1)S(1)}, bf16[3,512,512]{2,1,0:T(8,128)(2,1)}, u32[]{:S(2)}) %copy-start) | copy-done | bytes 1572888
  2.7 0.0 copy-start.2
  2.7 1.2 %copy-done.2 = bf16[32,128,128]{2,1,0:T(8,128)(2,1)S(1)} copy-done((bf16[32,128,128]{2,1,0:T(8,128)(2,1)S(1)}, bf16[32,128,128]{2,1,0:T(8,128)(2,1)}, u32[]{:S(2)}) %copy-start.2) | copy-done | bytes 1048600
  3.9 0.0 copy-start.3
  3.9 0.9 %copy-done.3 = bf16[128,512]{1,0:T(8,128)(2,1)S(1)} copy-done((bf16[128,512]{1,0:T(8,128)(2,1)S(1)}, bf16[128,512]{1,0:T(8,128)(2,1)}, u32[]{:S(2)}) %copy-start.3) | copy-done | bytes 131096
  4.8 0.0 copy-start.6
  4.8 0.9 %copy-done.6 = bf16[128,512]{1,0:T(8,128)(2,1)S(1)} copy-done((bf16[128,512]{1,0:T(8,128)(2,1)S(1)}, bf16[128,512]{1,0:T(8,128)(2,1)}, u32[]{:S(2)}) %copy-start.6) | copy-done | bytes 131096
  5.7 0.0 copy-start.8
  5.7 0.7 copy-done.8
  6.4 0.0 copy-start.10
  6.4 0.7 copy-done.10
  7.1 0.0 copy-start.1
  7.1 0.0 copy-start.4
  7.1 0.0 copy-start.5
  7.1 0.0 copy-start.7
  7.1 1.3 %prep.1 = (bf16[1024,512]{1,0:T(8,128)(2,1)S(1)}, bf16[2,128,256]{2,1,0:T(8,128)(2,1)S(1)}, bf16[4,256,128]{2,1,0:T(8,128)(2,1)S(1)}) custom-call(s32[2,32]{1,0:T(2,128)S(1)} %bitcast.1, s32[1]{0:T(128)S(6)} %copy.13.count, s32[32]{0:T(128)S(1)} %copy-done.8, bf16[32,128,128]{2,1,0:T(8,128)(2,1)S(1)} %copy-done.2, bf16[128,512]{1,0:T(8,128)(2,1)S(1)} %copy-done.3, ...), custom_call_target="tpu_custom_call" | custom-call | tf_op jit(solution)/shard_map/prep/pallas_call | solution.py:367
  8.4 0.0 copy-done.9
  8.4 0.1 copy-done.1
  8.5 0.0 copy-done.4
  8.5 0.1 copy-done.5
  8.6 0.0 copy-done.7
  8.7 68.8 %main.1 = (bf16[128,512]{1,0:T(8,128)(2,1)S(1)}, f32[128,512]{1,0:T(8,128)S(1)}, bf16[4,512,512]{2,1,0:T(8,128)(2,1)S(1)}) custom-call(s32[32]{0:T(128)S(1)} %copy-done.9, bf16[1024,512]{1,0:T(8,128)(2,1)S(1)} %get-tuple-element.10.adj, bf16[2,128,256]{2,1,0:T(8,128)(2,1)S(1)} %get-tuple-element.11.proj, bf16[4,256,128]{2,1,0:T(8,128)(2,1)S(1)} %get-tuple-element.12.chunks, ...), custom_call_target="tpu_custom_call" | custom-call | tf_op jit(solution)/shard_map/main/pallas_call | solution.py:384
  77.4 3.9 %post.1 = (bf16[128,512]{1,0:T(8,128)(2,1)}, f32[128,512]{1,0:T(8,128)}, f32[512,512]{1,0:T(8,128)}, f32[3,512,512]{2,1,0:T(8,128)}) custom-call(bf16[128,512]{1,0:T(8,128)(2,1)S(1)} %get-tuple-element.13.out_in, f32[128,512]{1,0:T(8,128)S(1)} %get-tuple-element.14.dims_in, bf16[4,512,512]{2,1,0:T(8,128)(2,1)S(1)} %get-tuple-element.15.weights), custom_call_target="tpu_custom_call" | custom-call | tf_op jit(solution)/shard_map/post/pallas_call | solution.py:427
Async XLA Ops:
  0.6 7.8 %copy-start.9 = (s32[32]{0:T(128)S(1)}, s32[32]{0:T(128)}, u32[]{:S(2)}) copy-start(s32[32]{0:T(128)} %table.3) | copy-start | bytes 388
  1.3 1.4 %copy-start = (bf16[3,512,512]{2,1,0:T(8,128)(2,1)S(1)}, bf16[3,512,512]{2,1,0:T(8,128)(2,1)}, u32[]{:S(2)}) copy-start(bf16[3,512,512]{2,1,0:T(8,128)(2,1)} %w_tables.3) | copy-start | bytes 4718596
  2.7 1.2 %copy-start.2 = (bf16[32,128,128]{2,1,0:T(8,128)(2,1)S(1)}, bf16[32,128,128]{2,1,0:T(8,128)(2,1)}, u32[]{:S(2)}) copy-start(bf16[32,128,128]{2,1,0:T(8,128)(2,1)} %tiles.1) | copy-start | bytes 3145732
  3.9 0.9 %copy-start.3 = (bf16[128,512]{1,0:T(8,128)(2,1)S(1)}, bf16[128,512]{1,0:T(8,128)(2,1)}, u32[]{:S(2)}) copy-start(bf16[128,512]{1,0:T(8,128)(2,1)} %facts.3) | copy-start | bytes 393220
  4.8 0.9 %copy-start.6 = (bf16[128,512]{1,0:T(8,128)(2,1)S(1)}, bf16[128,512]{1,0:T(8,128)(2,1)}, u32[]{:S(2)}) copy-start(bf16[128,512]{1,0:T(8,128)(2,1)} %dims.1) | copy-start | bytes 393220
  5.7 0.7 copy-start.8
  6.4 0.7 copy-start.10
  7.1 1.4 %copy-start.1 = (bf16[3,512,512]{2,1,0:T(8,128)(2,1)S(1)}, bf16[3,512,512]{2,1,0:T(8,128)(2,1)}, u32[]{:S(2)}) copy-start(bf16[3,512,512]{2,1,0:T(8,128)(2,1)} %w_tables.3) | copy-start | bytes 4718596
  7.1 1.4 %copy-start.4 = (bf16[128,512]{1,0:T(8,128)(2,1)S(1)}, bf16[128,512]{1,0:T(8,128)(2,1)}, u32[]{:S(2)}) copy-start(bf16[128,512]{1,0:T(8,128)(2,1)} %facts.3) | copy-start | bytes 393220
  7.1 1.5 %copy-start.5 = (bf16[512,512]{1,0:T(8,128)(2,1)S(1)}, bf16[512,512]{1,0:T(8,128)(2,1)}, u32[]{:S(2)}) copy-start(bf16[512,512]{1,0:T(8,128)(2,1)} %w_self.1) | copy-start | bytes 1572868
  7.1 1.6 %copy-start.7 = (bf16[128,512]{1,0:T(8,128)(2,1)S(1)}, bf16[128,512]{1,0:T(8,128)(2,1)}, u32[]{:S(2)}) copy-start(bf16[128,512]{1,0:T(8,128)(2,1)} %cot.1) | copy-start | bytes 393220
